TPU v7x, 512 devices: a whole 4x4x16 slice. The times are simulated.
512 devices in a mesh: dp: 16 (over x, y), expert: 32 (over z, core).
Axes of the slice: x: 4, y: 4, z: 16, core: 2. Of those that a mesh axis runs over, the one named last changes fastest.
Arguments:
- tokens: bfloat16 [65536, 2048], P(('dp', 'expert')), may hold values from -6 to 6
- cotangent: bfloat16 [65536, 2048], P(('dp', 'expert')), may hold values from -6 to 6
- routes: int32 [65536, 8], P(('dp', 'expert')), may hold values from 0 to 127, as said below
- slot_gates: float32 [65536, 8], P(('dp', 'expert')), may hold values from 0.05 to 0.5
- gate_up_weight: bfloat16 [32, 2, 2048, 768], P('expert', None, None, 'dp'), may hold values from -0.125 to 0.125
- down_master: float32 [32, 768, 2048], P('expert', 'dp'), may hold values from -0.21875 to 0.21875
- first_moment: float32 [32, 768, 2048], P('expert', 'dp'), may hold values from -4 to 4
- second_moment: float32 [32, 768, 2048], P('expert', 'dp'), may hold values from 0.5 to 4
Outputs:
- new_down: float32 [32, 768, 2048], P('expert', 'dp')
- new_first: float32 [32, 768, 2048], P('expert', 'dp')
- new_second: float32 [32, 768, 2048], P('expert', 'dp')
Inputs may be any that keep to these rules, and one draw needn't show every extreme that they name: `routes`: each row names 8 different experts. In the 128 rows of one device no expert is named more than 24 times; in every group of devices that share a dp index, one expert below 32 is named exactly 24 times by every device of the group.
All inputs are finite; a program needn't handle non-finite values.
Results may differ from a plain program's by a relative error of at most 0.025.
Values may be sent and summed in bfloat16 or wider, within the bound.
A program may use at most 64 MiB of HBM per device.

v0:
```python
import jax
import jax.numpy as jnp
from jax import lax
from jax.sharding import PartitionSpec as P

MOST = 24


BETA_ONE = 0.9
BETA_TWO = 0.95
LEARN_RATE = 0.003
DECAY_RATE = 0.1
ADAM_EPS = 1e-08


def pack_rows(features, cotangent, routes, slot_gates, experts, most):
    tok_rows = routes.shape[0]
    top_count = routes.shape[1]
    flat_routes = routes.reshape(-1)
    flat_gates = slot_gates.reshape(-1)
    expert_ids = jnp.arange(experts, dtype=jnp.int32)
    one_hot = (flat_routes[:, None] == expert_ids[None, :]).astype(jnp.int32)
    earlier = jnp.cumsum(one_hot, axis=0) - one_hot
    slot_rank = jnp.sum(earlier * one_hot, axis=1)
    in_window = flat_routes < experts
    slot_place = jnp.where(in_window, flat_routes * most + slot_rank, experts * most)
    slot_owner = jnp.arange(tok_rows * top_count, dtype=jnp.int32) // top_count
    slot_token = jnp.zeros((experts * most,), jnp.int32).at[slot_place].set(slot_owner, mode="drop")
    slot_weight = (
        jnp.zeros((experts * most,), flat_gates.dtype).at[slot_place].set(flat_gates, mode="drop")
    )
    slot_filled = jnp.zeros((experts * most,), jnp.int32).at[slot_place].set(1, mode="drop")
    picked = features[slot_token]
    rows_x = jnp.where(slot_filled[:, None] > 0, picked, jnp.zeros_like(picked))
    rows_c = (cotangent[slot_token].astype(jnp.float32) * slot_weight[:, None]).astype(jnp.bfloat16)
    model_width = features.shape[1]
    return (rows_x.reshape(experts, most, model_width), rows_c.reshape(experts, most, model_width))


def per_device(
    tokens, cotangent, routes, slot_gates, gate_up_weight, down_master, first_moment, second_moment
):
    experts = lax.axis_size("expert")
    model_width = tokens.shape[1]
    rows_x, rows_c = pack_rows(tokens, cotangent, routes, slot_gates, experts, MOST)
    recv_x = lax.all_to_all(rows_x, "expert", split_axis=0, concat_axis=0, tiled=True)
    flat_x = recv_x.reshape(-1, model_width)
    local_weight = gate_up_weight[0]
    whole_weight = lax.all_gather(local_weight, "dp", axis=2, tiled=True)
    projected = jnp.einsum("rd,gdc->rgc", flat_x, whole_weight, preferred_element_type=jnp.float32)
    hidden = (jax.nn.silu(projected[:, 0]) * projected[:, 1]).astype(jnp.bfloat16)
    recv_c = lax.all_to_all(rows_c, "expert", split_axis=0, concat_axis=0, tiled=True)
    flat_c = recv_c.reshape(-1, model_width)
    grad_share = lax.psum_scatter(
        lax.dot_general(
            hidden, flat_c, (((0,), (0,)), ((), ())), preferred_element_type=jnp.float32
        ).astype(jnp.bfloat16),
        "dp",
        scatter_dimension=0,
        tiled=True,
    ).astype(jnp.float32)
    master = down_master[0]
    new_first = BETA_ONE * first_moment[0] + (1.0 - BETA_ONE) * grad_share
    new_second = BETA_TWO * second_moment[0] + (1.0 - BETA_TWO) * grad_share * grad_share
    new_down = master - LEARN_RATE * (
        new_first / (jnp.sqrt(new_second) + ADAM_EPS) + DECAY_RATE * master
    )
    return (new_down[None], new_first[None], new_second[None])


def solution(mesh):
    return jax.shard_map(
        per_device,
        mesh=mesh,
        in_specs=(
            P(("dp", "expert"), None),
            P(("dp", "expert"), None),
            P(("dp", "expert"), None),
            P(("dp", "expert"), None),
            P("expert", None, None, "dp"),
            P("expert", "dp", None),
            P("expert", "dp", None),
            P("expert", "dp", None),
        ),
        out_specs=(P("expert", "dp", None), P("expert", "dp", None), P("expert", "dp", None)),
        check_vma=False,
    )
```

profile of v0, /device:TPU:1, one launch (start us, length us, event | category | flops | bytes accessed | tf_op | source)
XLA Modules:
  0.0 445.8 jit_solution(12316650651665774685)
XLA Ops:
  7.2 0.8 copy.22
  8.0 0.1 eq.29
  8.1 0.1 eq.25
  8.2 0.7 broadcast_multiply_fusion
  8.9 0.7 broadcast_compare_fusion
  9.6 9.0 %reduce-window.6 = s32[32,8,128]{2,1,0:T(8,128)S(1)} reduce-window(s32[32,8,128]{2,1,0:T(8,128)S(1)} %fusion.16, s32[]{:T(128)} %constant.19.clone.1), window={size=1x1x128 pad=0_0x0_0x127_0}, to_apply=%region_0.0 | reduce-window | flops 4161536 | bytes 262148 | tf_op jit(solution)/shard_map/reduce-window
  18.7 0.1 copy.24
  19.0 0.1 broadcast_add_fusion
  19.1 0.1 copy.21
  19.2 0.1 mul.83
  19.3 0.1 copy.20
  19.4 0.1 lt.34
  19.6 4.3 scatter_custom_fusion.1
  23.9 4.3 scatter_custom_fusion
  28.4 4.3 gather_fusion
  32.7 3.9 broadcast_select_fusion
  36.5 16.9 %all-to-all-start = ((bf16[32,24,2048]{2,1,0:T(8,128)(2,1)}), bf16[32,24,2048]{2,1,0:T(8,128)(2,1)}, u32[]{:S(2)}, u32[]{:S(2)}) async-start(bf16[32,24,2048]{2,1,0:T(8,128)(2,1)} %broadcast_select_fusion), calls=%async_computation | async-start | bytes 6291456 | tf_op jit(solution)/shard_map/all_to_all | solution.py:46
  53.5 1.2 copy.26
  54.7 4.2 gather_fusion.1
  59.0 0.1 copy.28
  59.1 0.1 reshape.140
  59.2 4.3 scatter_custom_fusion.2
  63.6 4.1 fusion
  67.7 126.8 %all-to-all-done = bf16[32,24,2048]{2,1,0:T(8,128)(2,1)} async-done(((bf16[32,24,2048]{2,1,0:T(8,128)(2,1)}), bf16[32,24,2048]{2,1,0:T(8,128)(2,1)}, u32[]{:S(2)}, u32[]{:S(2)}) %all-to-all-start) | async-done | bytes 3145760 | tf_op jit(solution)/shard_map/all_to_all | solution.py:46
  194.5 7.8 %all-to-all-start.1 = ((bf16[32,24,2048]{2,1,0:T(8,128)(2,1)}), bf16[32,24,2048]{2,1,0:T(8,128)(2,1)}, u32[]{:S(2)}, u32[]{:S(2)}) async-start(bf16[32,24,2048]{2,1,0:T(8,128)(2,1)} %fusion), calls=%async_computation.1 | async-start | bytes 6291456 | tf_op jit(solution)/shard_map/all_to_all | solution.py:52
  202.2 0.2 reduce-scatter.2.cloned.1.call-start
  202.5 16.1 %copy.27 = bf16[1,2,2048,768]{3,2,1,0:T(8,128)(2,1)} copy(bf16[1,2,2048,768]{2,1,0,3:T(2,128)(2,1)} %all-gather.3.cloned.1.call-done) | data formatting | bytes 12582912 | tf_op jit(solution)/shard_map/all_gather | solution.py:49
  218.6 9.5 %fusion.1 = f32[768,2,768]{2,0,1:T(8,128)} fusion(bf16[768,2048,1]{1,0,2:T(8,128)(2,1)} %bitcast.8, bf16[1,2,2048,768]{3,2,1,0:T(8,128)(2,1)} %copy.27), kind=kOutput, calls=%fused_computation.7 | convolution fusion | flops 4831838208 | bytes 14155776 | tf_op jit(solution)/shard_map/rd,gdc->rgc/dot_general | solution.py:50
  228.2 115.2 %all-to-all-done.1 = bf16[32,24,2048]{2,1,0:T(8,128)(2,1)} async-done(((bf16[32,24,2048]{2,1,0:T(8,128)(2,1)}), bf16[32,24,2048]{2,1,0:T(8,128)(2,1)}, u32[]{:S(2)}, u32[]{:S(2)}) %all-to-all-start.1) | async-done | bytes 3145760 | tf_op jit(solution)/shard_map/all_to_all | solution.py:52
  343.4 7.7 %convolution_convert_fusion = bf16[768,2048]{1,0:T(8,128)(2,1)} fusion(bf16[768,2048]{1,0:T(8,128)(2,1)} %bitcast.12, f32[768,2,768]{2,0,1:T(8,128)} %fusion.1), kind=kOutput, calls=%fused_computation.9 | convolution fusion | flops 2421030912 | bytes 11010048 | tf_op jit(solution)/shard_map/dot_general | solution.py:55
  351.1 85.6 %reduce-scatter.2.cloned.1.call-done = bf16[48,2048]{1,0:T(8,128)(2,1)} async-done(((bf16[768,2048]{1,0:T(8,128)(2,1)}), bf16[48,2048]{1,0:T(8,128)(2,1)}) %reduce-scatter.2.cloned.1.call-update) | async-done | bytes 196624 | tf_op jit(solution)/shard_map/reduce_scatter | solution.py:54
  436.7 2.2 fusion.12
  (32 shorter events, 0.6 us)
Async XLA Ops:
  7.2 21.2 %copy-start = (bf16[128,2048]{1,0:T(8,128)(2,1)S(1)}, bf16[128,2048]{1,0:T(8,128)(2,1)}, u32[]{:S(2)}) copy-start(bf16[128,2048]{1,0:T(8,128)(2,1)} %param.8) | copy-start | bytes 1572868
  36.5 17.0 %copy-start.5 = (bf16[1,2,2048,48]{2,3,1,0:T(8,128)(2,1)S(1)}, bf16[1,2,2048,48]{2,3,1,0:T(8,128)(2,1)}, u32[]{:S(2)}) copy-start(bf16[1,2,2048,48]{2,3,1,0:T(8,128)(2,1)} %param.12) | copy-start | bytes 1179652
  36.5 18.2 %copy-start.1 = (bf16[128,2048]{1,0:T(8,128)(2,1)S(1)}, bf16[128,2048]{1,0:T(8,128)(2,1)}, u32[]{:S(2)}) copy-start(bf16[128,2048]{1,0:T(8,128)(2,1)} %param.9) | copy-start | bytes 1572868
  36.5 157.9 %all-to-all-start = ((bf16[32,24,2048]{2,1,0:T(8,128)(2,1)}), bf16[32,24,2048]{2,1,0:T(8,128)(2,1)}, u32[]{:S(2)}, u32[]{:S(2)}) async-start(bf16[32,24,2048]{2,1,0:T(8,128)(2,1)} %broadcast_select_fusion), calls=%async_computation | async-start | bytes 6291456 | tf_op jit(solution)/shard_map/all_to_all | solution.py:46
  53.5 149.0 %all-gather.3.cloned.1.call-start = ((), (), s32[]{:S(2)}) async-start(), calls=%async_computation.4 | async-start | bytes 6684672 | tf_op jit(solution)/shard_map/all_gather | solution.py:49
  54.7 4.3 copy-start.6
  194.5 148.9 %all-to-all-start.1 = ((bf16[32,24,2048]{2,1,0:T(8,128)(2,1)}), bf16[32,24,2048]{2,1,0:T(8,128)(2,1)}, u32[]{:S(2)}, u32[]{:S(2)}) async-start(bf16[32,24,2048]{2,1,0:T(8,128)(2,1)} %fusion), calls=%async_computation.1 | async-start | bytes 6291456 | tf_op jit(solution)/shard_map/all_to_all | solution.py:52
  202.2 234.5 %reduce-scatter.2.cloned.1.call-start = ((), (), s32[]{:S(2)}) async-start(), calls=%async_computation.3 | async-start | bytes 3342336 | tf_op jit(solution)/shard_map/reduce_scatter | solution.py:54
  351.0 85.7 %copy-start.2 = (f32[1,48,2048]{2,1,0:T(8,128)S(1)}, f32[1,48,2048]{2,1,0:T(8,128)}, u32[]{:S(2)}) copy-start(f32[1,48,2048]{2,1,0:T(8,128)} %param.15) | copy-start | bytes 1179652
  351.0 85.7 %copy-start.3 = (f32[1,48,2048]{2,1,0:T(8,128)S(1)}, f32[1,48,2048]{2,1,0:T(8,128)}, u32[]{:S(2)}) copy-start(f32[1,48,2048]{2,1,0:T(8,128)} %param.14) | copy-start | bytes 1179652
  351.0 85.7 %copy-start.4 = (f32[1,48,2048]{2,1,0:T(8,128)S(1)}, f32[1,48,2048]{2,1,0:T(8,128)}, u32[]{:S(2)}) copy-start(f32[1,48,2048]{2,1,0:T(8,128)} %param.13) | copy-start | bytes 1179652
Sparse Core Ops, SparseCore 0:
  57.9 77.1 all-gather.2
  351.2 85.4 reduce-scatter.1
where the time goes:
time: 447 us; the launch traced here: 446 us
  waiting for transfers between devices  328 us (73%)
  local copies, waits for them, and re-layouts  40.9 us (9%)
  starting transfers between devices  25 us (6%)
  other arithmetic  20.8 us (5%)
  matrix products  17.2 us (4%)
  between operations  14.2 us (3%)
    all_to_all x1, waiting for transfers between devices, per_device(): lax.all_to_all(rows_x, 'expert', split_axis=0, concat_axis=0, tiled=True)  127 us
    all_to_all x1, waiting for transfers between devices, per_device(): lax.all_to_all(rows_c, 'expert', split_axis=0, concat_axis=0, tiled=True)  115 us
    reduce_scatter x1, waiting for transfers between devices, per_device(): lax.psum_scatter(lax.dot_general(hidden, flat_c, (((0,), (0,)), ((), ()))...  85.6 us
    all_to_all x1, starting transfers between devices, per_device(): lax.all_to_all(rows_x, 'expert', split_axis=0, concat_axis=0, tiled=True)  16.9 us
    all_gather x1, local copies, waits for them, and re-layouts, per_device(): whole_weight = lax.all_gather(local_weight, 'dp', axis=2, tiled=True)  16.1 us
    dot_general x1, matrix products, per_device(): jnp.einsum('rd,gdc->rgc', flat_x, whole_weight, preferred_element_type=jn...  9.55 us
    another operation x3, other arithmetic  9.15 us
  transfers between devices with their start and end apart: 4, of which 3 were waited for; matrix products, arithmetic and copies ran while one was open for 9% of the time, Pallas kernels for 0%

commit v1 on v0

v1 whole, which is shorter than its diff:
```python
import functools

import jax
import jax.numpy as jnp
from jax import lax
from jax.experimental import pallas as pl
from jax.experimental.pallas import tpu as pltpu
from jax.sharding import PartitionSpec as P

MOST = 24
NQ = 4
OFFSETS = (0, 0, 1, 1)

BETA_ONE = 0.9
BETA_TWO = 0.95
LEARN_RATE = 0.003
DECAY_RATE = 0.1
ADAM_EPS = 1e-08

MESH = pl.DeviceIdType.MESH
F32 = jnp.float32
BF16 = jnp.bfloat16


def kernel(
    ndp, ne,
    x_ref, c_ref, rt_ref, gt_ref, w_ref,
    grad_ref,
    buf, w_all, g_all, p_all, gate_all, rows, ht, ps, land,
    loc_sem, rr, rs, pr, psd, wr, ws, lr_sem, ls_sem,
):
    nz = ne // 2
    items = 2 * NQ
    hops = nz // 2 + 1
    toks = buf.shape[2]
    cw = buf.shape[3]
    width = NQ * cw
    pair = 2 * MOST
    nrows = nz * pair
    fd = w_ref.shape[1]
    ff = ndp * fd

    me = lax.axis_index("expert")
    dp = lax.axis_index("dp")
    z = me // 2
    core = me % 2
    partner = me + 1 - 2 * core

    def zslot(d):
        return 2 * ((z + d + nz) % nz) + core

    def load(k, t, q):
        src = x_ref if t == 0 else c_ref
        return pltpu.make_async_copy(
            src.at[:, pl.ds(q * cw, cw)], buf.at[k, me], loc_sem.at[k]
        )

    for q in range(NQ):
        load(q, 0, q).start()
    for q in range(NQ):
        load(NQ + q, 1, q).start()
    w_load = pltpu.make_async_copy(w_ref, w_all.at[:, dp], loc_sem.at[items])
    w_load.start()

    expert_id = lax.broadcasted_iota(jnp.int32, (ne, toks), 0)
    table = jnp.zeros((ne, toks), F32)
    for k in range(rt_ref.shape[0]):
        table = table + jnp.where(rt_ref[k : k + 1, :] == expert_id, gt_ref[k : k + 1, :], 0.0)
    g_all[me] = table

    barrier = pltpu.get_barrier_semaphore()
    for other in (zslot(1), zslot(-1), partner):
        pl.semaphore_signal(barrier, inc=1, device_id={"expert": other}, device_id_type=MESH)

    @pl.loop(1, ndp)
    def _(d):
        pl.semaphore_signal(
            barrier, inc=1, device_id={"dp": (dp + d) % ndp}, device_id_type=MESH
        )

    pl.semaphore_wait(barrier, 3 + ndp - 1)

    def chunk(k, s):
        return g_all.at[s] if k is None else buf.at[k, s]

    def sidx(k):
        return items if k is None else k

    def ring_copy(k, direction, s, h):
        return pltpu.make_async_remote_copy(
            src_ref=chunk(k, s), dst_ref=chunk(k, s),
            send_sem=rs.at[sidx(k), direction, h],
            recv_sem=rr.at[sidx(k), direction, h + 1],
            device_id={"expert": zslot(1 if direction == 0 else -1)},
            device_id_type=MESH,
        )

    def ring_arrived(k, direction, s, h):
        pltpu.make_async_remote_copy(
            src_ref=chunk(k, s), dst_ref=chunk(k, s),
            send_sem=rs.at[sidx(k), direction, h],
            recv_sem=rr.at[sidx(k), direction, h],
            device_id={"expert": zslot(1 if direction == 0 else -1)},
            device_id_type=MESH,
        ).wait_recv()

    def partner_copy(k, s, zz):
        return pltpu.make_async_remote_copy(
            src_ref=chunk(k, s), dst_ref=chunk(k, s),
            send_sem=psd.at[sidx(k), zz], recv_sem=pr.at[sidx(k), zz],
            device_id={"expert": partner}, device_id_type=MESH,
        )

    def reach(parity, direction):
        return nz // 2 if parity == direction else nz // 2 - 1

    def event(k, parity, h, ready):
        @pl.when(h == 0)
        def _():
            ready()
            ring_copy(k, 0, me, 0).start()
            ring_copy(k, 1, me, 0).start()
            partner_copy(k, me, z).start()

        for direction in range(2):
            last = reach(parity, direction)

            @pl.when((h > 0) & (h <= last))
            def _():
                d = -h if direction == 0 else h
                s = zslot(d)
                ring_arrived(k, direction, s, h)

                @pl.when(h < last)
                def _():
                    ring_copy(k, direction, s, h).start()

                partner_copy(k, s, s // 2).start()

    def pairs(k, parity, h, work):
        def one(zz):
            partner_copy(k, 2 * zz + 1 - core, zz).wait_recv()
            work(zz)

        @pl.when(h == 0)
        def _():
            one(z)

        for direction in range(2):
            @pl.when((h > 0) & (h <= reach(parity, direction)))
            def _():
                one(zslot(-h if direction == 0 else h) // 2)

    def build(zz):
        both = jnp.concatenate(
            [g_all[2 * zz, pl.ds(me, 1), :], g_all[2 * zz + 1, pl.ds(me, 1), :]], axis=0
        )
        mask = jnp.where(both > 0.0, 1.0, 0.0)
        row_id = lax.broadcasted_iota(jnp.int32, (toks, toks), 0)
        col_id = lax.broadcasted_iota(jnp.int32, (toks, toks), 1)
        before = jnp.where(row_id < col_id, 1.0, 0.0).astype(BF16)
        padded = jnp.concatenate([mask, jnp.zeros((6, toks), F32)], axis=0)
        rank = jnp.dot(padded.astype(BF16), before, preferred_element_type=F32)
        places = []
        for s in range(2):
            places.append(
                jnp.where(mask[s : s + 1, :] > 0.0, rank[s : s + 1, :] + float(MOST * s), -1.0)
            )
        place = jnp.concatenate(places, axis=1)
        gates = jnp.concatenate([both[0:1, :], both[1:2, :]], axis=1)
        wanted = lax.broadcasted_iota(jnp.int32, (pair, 2 * toks), 0).astype(F32)
        hit = wanted == place
        p_all[zz] = jnp.where(hit, 1.0, 0.0).astype(BF16)
        gate = jnp.sum(jnp.where(hit, gates, 0.0), axis=1, keepdims=True)
        gate_all[zz] = jnp.broadcast_to(gate, (pair, 128))

    def select(k, zz):
        both = buf[k, pl.ds(2 * zz, 2)].reshape(2 * toks, cw)
        got = jnp.dot(p_all[zz], both, preferred_element_type=F32)
        gate = gate_all[zz][:, 0:1]
        scale = jnp.where(k >= NQ, gate, jnp.ones_like(gate))
        rows[k, pl.ds(pl.multiple_of(zz * pair, 16), pair), :] = (got * scale).astype(BF16)

    fsplit = 2
    fb = ff // fsplit
    rb = 256 if nrows % 256 == 0 else nrows
    rsplit = nrows // rb
    pieces = fsplit * rsplit

    def nt(a, b):
        return lax.dot_general(a, b, (((1,), (1,)), ((), ())), preferred_element_type=F32)

    def hidden_piece(p):
        f0 = p // rsplit
        r0 = p % rsplit
        gate = jnp.zeros((fb, rb), F32)
        up = jnp.zeros((fb, rb), F32)
        for q in range(NQ):
            xs = rows[q, pl.ds(pl.multiple_of(r0 * rb, 16), rb), :]
            blocks = pl.ds(f0 * (ndp // fsplit), ndp // fsplit)
            cols = pl.ds(q * cw, cw)
            gate = gate + nt(w_all[0, blocks, :, cols].reshape(fb, cw), xs)
            up = up + nt(w_all[1, blocks, :, cols].reshape(fb, cw), xs)
        act = gate / (1.0 + jnp.exp(-gate)) * up
        ht[pl.ds(pl.multiple_of(f0 * fb, 16), fb), pl.ds(pl.multiple_of(r0 * rb, 128), rb)] = act.astype(BF16)

    def w_copy(other, slot):
        return pltpu.make_async_remote_copy(
            src_ref=w_all.at[:, slot], dst_ref=w_all.at[:, slot],
            send_sem=ws.at[other], recv_sem=wr.at[slot],
            device_id={"dp": other}, device_id_type=MESH,
        )

    def r_copy(q, other, slot):
        return pltpu.make_async_remote_copy(
            src_ref=ps.at[q, other], dst_ref=land.at[q, slot],
            send_sem=ls_sem.at[q, other], recv_sem=lr_sem.at[q, slot],
            device_id={"dp": other}, device_id_type=MESH,
        )

    def partial(q):
        for f0 in range(fsplit):
            part = jnp.dot(
                ht[f0 * fb : (f0 + 1) * fb, :], rows[NQ + q], preferred_element_type=F32
            )
            per = ndp // fsplit
            ps[q, f0 * per : (f0 + 1) * per] = part.astype(BF16).reshape(per, fd, cw)
        land[q, dp] = ps[q, dp]

        @pl.loop(1, ndp)
        def _(d):
            r_copy(q, (dp + d) % ndp, dp).start()

    x_done = max(OFFSETS) + hops

    @pl.loop(0, 2 * hops + max(OFFSETS) + 1)
    def _(r):
        @pl.when(r < hops)
        def _():
            event(None, 0, r, lambda: None)

        for j in range(NQ):
            lr = r - OFFSETS[j]

            @pl.when((lr >= 0) & (lr < 2 * hops))
            def _():
                second = lr // hops
                k = j + NQ * second
                event(k, j % 2, lr % hops, lambda: load(k, 0, j).wait())

        @pl.when(r == 0)
        def _():
            w_load.wait()

            @pl.loop(1, ndp)
            def _(d):
                w_copy((dp + d) % ndp, dp).start()

        @pl.when(r == x_done + 1)
        def _():
            @pl.loop(1, ndp)
            def _(d):
                other = (dp + d) % ndp
                w_copy(other, other).wait_recv()

        @pl.when((r > x_done) & (r <= x_done + pieces))
        def _():
            hidden_piece(r - x_done - 1)

        @pl.when((r >= 1) & (r <= hops))
        def _():
            pairs(None, 0, r - 1, build)

        for j in range(NQ):
            late = r - 1 - OFFSETS[j]

            @pl.when((late >= 0) & (late < 2 * hops))
            def _():
                k = j + NQ * (late // hops)
                pairs(k, j % 2, late % hops, functools.partial(select, k))

            @pl.when(late == 2 * hops - 1)
            def _():
                partial(j)

    for q in range(NQ):
        @pl.loop(1, ndp)
        def _(d):
            other = (dp + d) % ndp
            r_copy(q, other, other).wait_recv()

        total = land[q, 0].astype(F32)
        for i in range(1, ndp):
            total = total + land[q, i].astype(F32)
        grad_ref[:, q * cw : (q + 1) * cw] = total

    def drain(k, parity):
        for direction in range(2):
            @pl.loop(0, reach(parity, direction))
            def _(h):
                ring_copy(k, direction, me, h).wait_send()

        @pl.loop(0, nz)
        def _(zz):
            partner_copy(k, me, zz).wait_send()

    drain(None, 0)

    @pl.loop(0, items // 2)
    def _(half):
        for parity in range(2):
            drain(2 * half + parity, parity)

    @pl.loop(1, ndp)
    def _(d):
        other = (dp + d) % ndp
        w_copy(other, dp).wait_send()
        for q in range(NQ):
            r_copy(q, other, dp).wait_send()


def grad_kernel(mesh, tokens, cotangent, routes_t, gates_t, weight):
    ndp = mesh.shape["dp"]
    ne = mesh.shape["expert"]
    nz = ne // 2
    toks, width = tokens.shape
    cw = width // NQ
    fd = weight.shape[1]
    items = 2 * NQ
    hops = nz // 2 + 1
    nrows = ne * MOST
    dma = pltpu.SemaphoreType.DMA
    anywhere = pl.BlockSpec(memory_space=pl.ANY)
    vmem = pl.BlockSpec(memory_space=pltpu.VMEM)
    return pl.pallas_call(
        functools.partial(kernel, ndp, ne),
        out_shape=jax.ShapeDtypeStruct((fd, width), F32),
        in_specs=[anywhere, anywhere, vmem, vmem, anywhere],
        out_specs=vmem,
        scratch_shapes=[
            pltpu.VMEM((items, ne, toks, cw), BF16),
            pltpu.VMEM((2, ndp, fd, width), BF16),
            pltpu.VMEM((ne, ne, toks), F32),
            pltpu.VMEM((nz, 2 * MOST, 2 * toks), BF16),
            pltpu.VMEM((nz, 2 * MOST, 128), F32),
            pltpu.VMEM((items, nrows, cw), BF16),
            pltpu.VMEM((ndp * fd, nrows), BF16),
            pltpu.VMEM((NQ, ndp, fd, cw), BF16),
            pltpu.VMEM((NQ, ndp, fd, cw), BF16),
            dma((items + 1,)),
            dma((items + 1, 2, hops)),
            dma((items + 1, 2, hops)),
            dma((items + 1, nz)),
            dma((items + 1, nz)),
            dma((ndp,)),
            dma((ndp,)),
            dma((NQ, ndp)),
            dma((NQ, ndp)),
        ],
        compiler_params=pltpu.CompilerParams(
            collective_id=0, has_side_effects=True, vmem_limit_bytes=67043328
        ),
        name="expert_grad",
    )(tokens, cotangent, routes_t, gates_t, weight)


def solution(mesh):
    def per_device(
        tokens, cotangent, routes, slot_gates, gate_up_weight, down_master, first_moment, second_moment
    ):
        grad = grad_kernel(
            mesh, tokens, cotangent, routes.T, slot_gates.T, jnp.swapaxes(gate_up_weight[0], 1, 2)
        )
        master = down_master[0]
        new_first = BETA_ONE * first_moment[0] + (1.0 - BETA_ONE) * grad
        new_second = BETA_TWO * second_moment[0] + (1.0 - BETA_TWO) * grad * grad
        new_down = master - LEARN_RATE * (
            new_first / (jnp.sqrt(new_second) + ADAM_EPS) + DECAY_RATE * master
        )
        return (new_down[None], new_first[None], new_second[None])

    return jax.shard_map(
        per_device,
        mesh=mesh,
        in_specs=(
            P(("dp", "expert"), None),
            P(("dp", "expert"), None),
            P(("dp", "expert"), None),
            P(("dp", "expert"), None),
            P("expert", None, None, "dp"),
            P("expert", "dp", None),
            P("expert", "dp", None),
            P("expert", "dp", None),
        ),
        out_specs=(P("expert", "dp", None), P("expert", "dp", None), P("expert", "dp", None)),
        check_vma=False,
    )
```

time: 447 us -> 263 us (0.59)
  waiting for transfers between devices: 328 us -> 0 us
  Pallas kernels: 0 us -> 255 us
  local copies, waits for them, and re-layouts: 40.9 us -> 0 us
  starting transfers between devices: 25 us -> 0 us
  other arithmetic: 20.8 us -> 2.62 us
  matrix products: 17.2 us -> 0 us
  between operations: 14.2 us -> 0.64 us
    pallas_call x0 -> x1, Pallas kernels: none -> 255 us  [grad_kernel(): pl.pallas_call(functools.partial(kernel, ndp, ne), out_shape=jax.ShapeDty...]
    all_to_all x2 -> x0, waiting for transfers between devices: 242 us -> none  [the longest x1 127 us: per_device(): lax.all_to_all(rows_x, 'expert', split_axis=0, concat_axis=0, tiled=True)]
    reduce_scatter x1 -> x0, waiting for transfers between devices: 85.6 us -> none  [per_device(): lax.psum_scatter(lax.dot_general(hidden, flat_c, (((0,), (0,)), ((), ()))...]
    all_to_all x2 -> x0, starting transfers between devices: 24.7 us -> none  [the longest x1 16.9 us: per_device(): lax.all_to_all(rows_x, 'expert', split_axis=0, concat_axis=0, tiled=True)]
    dot_general x2 -> x0, matrix products: 17.2 us -> none  [the longest x1 9.55 us: per_device(): jnp.einsum('rd,gdc->rgc', flat_x, whole_weight, preferred_element_type=jn...]
    all_gather x1 -> x0, local copies, waits for them, and re-layouts: 16.1 us -> none  [per_device(): whole_weight = lax.all_gather(local_weight, 'dp', axis=2, tiled=True)]
    scatter x3 -> x0, local copies, waits for them, and re-layouts: 12.9 us -> none  [the longest x1 4.31 us: pack_rows(): jnp.zeros((experts * most,), jnp.int32).at[slot_place]]
    another operation x3 -> x0, other arithmetic: 9.15 us -> none
  transfers between devices with their start and end apart: 4 -> 0, of which waited for: 3 -> 0; matrix products, arithmetic and copies ran while one was open for 9% -> 0% of each run, Pallas kernels for 0% -> 0%
where the time goes in v1:
time: 263 us; the launch traced here: 258 us
  Pallas kernels  255 us (97%)
    pallas_call x1, Pallas kernels, grad_kernel(): pl.pallas_call(functools.partial(kernel, ndp, ne), out_shape=jax.ShapeDty...  255 us

profile of v1, /device:TPU:1, one launch (start us, length us, event | category | flops | bytes accessed | tf_op | source)
XLA Modules:
  0.0 258.4 jit_solution(16856067596417986534)
XLA Ops:
  0.6 255.1 %expert_grad.1 = f32[48,2048]{1,0:T(8,128)} custom-call(bf16[128,2048]{1,0:T(8,128)(2,1)} %x_ref.1, bf16[128,2048]{1,0:T(8,128)(2,1)} %c_ref.1, s32[8,128]{1,0:T(8,128)} %bitcast.35, f32[8,128]{1,0:T(8,128)} %bitcast.36, bf16[2,48,2048]{2,1,0:T(8,128)(2,1)} %bitcast.34), custom_call_target="tpu_custom_call" | custom-call | tf_op jit(solution)/shard_map/expert_grad/pallas_call | solution.py:335
  255.8 2.6 %fusion.5 = (f32[1,48,2048]{2,1,0:T(8,128)}, f32[1,48,2048]{2,1,0:T(8,128)}, f32[1,48,2048]{2,1,0:T(8,128)}) fusion(f32[48,2048]{1,0:T(8,128)} %expert_grad.1, f32[1,48,2048]{2,1,0:T(8,128)} %param.15, f32[1,48,2048]{2,1,0:T(8,128)} %param.14, f32[1,48,2048]{2,1,0:T(8,128)} %param.13), kind=kLoop, calls=%fused_computation.9 | loop fusion | flops 1277952 | bytes 2752512 | tf_op jit(solution)/shard_map/broadcast_in_dim | solution.py:380

commit v2 on v1

--- a/solution.py
+++ b/solution.py
@@ -9,7 +9,12 @@
 
 MOST = 24
 NQ = 4
-OFFSETS = (0, 0, 1, 1)
+C_START = (0, 1, 3, 5)
+SIDE = 4
+PEER_ORDER = (
+    (0, 1), (1, 0), (0, -1), (-1, 0), (1, 1), (-1, -1), (1, -1), (-1, 1),
+    (0, 2), (2, 0), (1, 2), (2, 1), (-1, 2), (2, -1), (2, 2),
+)
 
 BETA_ONE = 0.9
 BETA_TWO = 0.95
@@ -26,8 +31,8 @@
     ndp, ne,
     x_ref, c_ref, rt_ref, gt_ref, w_ref,
     grad_ref,
-    buf, w_all, g_all, p_all, gate_all, rows, ht, ps, land,
-    loc_sem, rr, rs, pr, psd, wr, ws, lr_sem, ls_sem,
+    buf, w_all, g_all, p_all, gate_all, rows, ht, ps, land, pm, po, pin,
+    loc_sem, rr, rs, pr, psd, wr, ws, lr_sem, ls_sem, pos, pfs, pps,
 ):
     nz = ne // 2
     items = 2 * NQ
@@ -39,6 +44,7 @@
     nrows = nz * pair
     fd = w_ref.shape[1]
     ff = ndp * fd
+    side = SIDE
 
     me = lax.axis_index("expert")
     dp = lax.axis_index("dp")
@@ -89,7 +95,7 @@
     def ring_copy(k, direction, s, h):
         return pltpu.make_async_remote_copy(
             src_ref=chunk(k, s), dst_ref=chunk(k, s),
-            send_sem=rs.at[sidx(k), direction, h],
+            send_sem=rs.at[sidx(k), direction],
             recv_sem=rr.at[sidx(k), direction, h + 1],
             device_id={"expert": zslot(1 if direction == 0 else -1)},
             device_id_type=MESH,
@@ -98,7 +104,7 @@
     def ring_arrived(k, direction, s, h):
         pltpu.make_async_remote_copy(
             src_ref=chunk(k, s), dst_ref=chunk(k, s),
-            send_sem=rs.at[sidx(k), direction, h],
+            send_sem=rs.at[sidx(k), direction],
             recv_sem=rr.at[sidx(k), direction, h],
             device_id={"expert": zslot(1 if direction == 0 else -1)},
             device_id_type=MESH,
@@ -107,12 +113,42 @@
     def partner_copy(k, s, zz):
         return pltpu.make_async_remote_copy(
             src_ref=chunk(k, s), dst_ref=chunk(k, s),
-            send_sem=psd.at[sidx(k), zz], recv_sem=pr.at[sidx(k), zz],
+            send_sem=psd.at[sidx(k)], recv_sem=pr.at[sidx(k), zz],
             device_id={"expert": partner}, device_id_type=MESH,
         )
 
     def reach(parity, direction):
         return nz // 2 if parity == direction else nz // 2 - 1
+
+    def full_reach(k, parity, direction):
+        return reach(parity, direction) - (0 if k is None else 2)
+
+    def packed_copy(k, direction, src, dst, sem, h):
+        return pltpu.make_async_remote_copy(
+            src_ref=src, dst_ref=dst, send_sem=sem.at[k, direction],
+            recv_sem=rr.at[k, direction, h],
+            device_id={"expert": zslot(1 if direction == 0 else -1)},
+            device_id_type=MESH,
+        )
+
+    def packed_first(k, parity, direction):
+        return packed_copy(
+            k, direction, po.at[k, direction], pin.at[k, direction, pl.ds(0, 2), core],
+            pos, reach(parity, direction) - 1,
+        )
+
+    def packed_second(k, parity, direction):
+        return packed_copy(
+            k, direction, pin.at[k, direction, 1, core], pin.at[k, direction, 2, core],
+            pfs, reach(parity, direction),
+        )
+
+    def packed_partner(k, direction, slot, zz, side_core):
+        ref = pin.at[k, direction, slot, side_core]
+        return pltpu.make_async_remote_copy(
+            src_ref=ref, dst_ref=ref, send_sem=pps.at[k], recv_sem=pr.at[k, zz],
+            device_id={"expert": partner}, device_id_type=MESH,
+        )
 
     def event(k, parity, h, ready):
         @pl.when(h == 0)
@@ -123,12 +159,11 @@
             partner_copy(k, me, z).start()
 
         for direction in range(2):
-            last = reach(parity, direction)
+            last = full_reach(k, parity, direction)
+            s = zslot(-h if direction == 0 else h)
 
             @pl.when((h > 0) & (h <= last))
             def _():
-                d = -h if direction == 0 else h
-                s = zslot(d)
                 ring_arrived(k, direction, s, h)
 
                 @pl.when(h < last)
@@ -137,7 +172,33 @@
 
                 partner_copy(k, s, s // 2).start()
 
-    def pairs(k, parity, h, work):
+            if k is not None:
+                @pl.when(h == last)
+                def _():
+                    few = jnp.dot(
+                        pm[direction, int(parity == direction)], buf[k, s],
+                        preferred_element_type=F32,
+                    )
+                    po[k, direction] = few.astype(BF16).reshape(2, pair, cw)
+
+                @pl.when(h == last + 1)
+                def _():
+                    packed_first(k, parity, direction).wait_recv()
+                    packed_second(k, parity, direction).start()
+                    packed_partner(k, direction, 0, s // 2, core).start()
+
+                @pl.when(h == last + 2)
+                def _():
+                    packed_second(k, parity, direction).wait_recv()
+                    packed_partner(k, direction, 2, s // 2, core).start()
+
+    def send_packed(k, parity, h):
+        for direction in range(2):
+            @pl.when(h == full_reach(k, parity, direction))
+            def _():
+                packed_first(k, parity, direction).start()
+
+    def pairs(k, parity, h, work, packed_work):
         def one(zz):
             partner_copy(k, 2 * zz + 1 - core, zz).wait_recv()
             work(zz)
@@ -147,20 +208,48 @@
             one(z)
 
         for direction in range(2):
-            @pl.when((h > 0) & (h <= reach(parity, direction)))
+            last = full_reach(k, parity, direction)
+            zz = zslot(-h if direction == 0 else h) // 2
+
+            @pl.when((h > 0) & (h <= last))
             def _():
-                one(zslot(-h if direction == 0 else h) // 2)
+                one(zz)
+
+            if k is not None:
+                for slot in (0, 2):
+                    @pl.when(h == last + 1 + slot // 2)
+                    def _():
+                        packed_partner(k, direction, slot, zz, 1 - core).wait_recv()
+                        packed_work(zz, direction, slot)
+
+    def ranks(mask):
+        row_id = lax.broadcasted_iota(jnp.int32, (toks, toks), 0)
+        col_id = lax.broadcasted_iota(jnp.int32, (toks, toks), 1)
+        before = jnp.where(row_id < col_id, 1.0, 0.0).astype(BF16)
+        padded = jnp.concatenate([mask, jnp.zeros((8 - mask.shape[0], toks), F32)], axis=0)
+        return jnp.dot(padded.astype(BF16), before, preferred_element_type=F32)
+
+    def build_pack(direction, long, s):
+        parts = []
+        for ahead in (1, 2):
+            dest = zslot(ahead if direction == 0 else -ahead) // 2
+            for other in range(2):
+                parts.append(g_all[s, pl.ds(2 * dest + other, 1), :])
+        mask = jnp.where(jnp.concatenate(parts, axis=0) > 0.0, 1.0, 0.0)
+        rank = ranks(mask)
+        wanted = lax.broadcasted_iota(jnp.int32, (2 * pair, toks), 0).astype(F32)
+        total = jnp.zeros((2 * pair, toks), F32)
+        for i in range(4):
+            place = jnp.where(mask[i : i + 1, :] > 0.0, rank[i : i + 1, :] + float(MOST * i), -1.0)
+            total = total + jnp.where(wanted == place, 1.0, 0.0)
+        pm[direction, long] = total.astype(BF16)
 
     def build(zz):
         both = jnp.concatenate(
             [g_all[2 * zz, pl.ds(me, 1), :], g_all[2 * zz + 1, pl.ds(me, 1), :]], axis=0
         )
         mask = jnp.where(both > 0.0, 1.0, 0.0)
-        row_id = lax.broadcasted_iota(jnp.int32, (toks, toks), 0)
-        col_id = lax.broadcasted_iota(jnp.int32, (toks, toks), 1)
-        before = jnp.where(row_id < col_id, 1.0, 0.0).astype(BF16)
-        padded = jnp.concatenate([mask, jnp.zeros((6, toks), F32)], axis=0)
-        rank = jnp.dot(padded.astype(BF16), before, preferred_element_type=F32)
+        rank = ranks(mask)
         places = []
         for s in range(2):
             places.append(
@@ -174,12 +263,22 @@
         gate = jnp.sum(jnp.where(hit, gates, 0.0), axis=1, keepdims=True)
         gate_all[zz] = jnp.broadcast_to(gate, (pair, 128))
 
-    def select(k, zz):
-        both = buf[k, pl.ds(2 * zz, 2)].reshape(2 * toks, cw)
-        got = jnp.dot(p_all[zz], both, preferred_element_type=F32)
+    def keep(k, zz, got):
         gate = gate_all[zz][:, 0:1]
         scale = jnp.where(k >= NQ, gate, jnp.ones_like(gate))
         rows[k, pl.ds(pl.multiple_of(zz * pair, 16), pair), :] = (got * scale).astype(BF16)
+
+    def select(k, zz):
+        both = buf[k, pl.ds(2 * zz, 2)].reshape(2 * toks, cw)
+        keep(k, zz, jnp.dot(p_all[zz], both, preferred_element_type=F32))
+
+    def select_packed(k, zz, direction, slot):
+        both = pin[k, direction, slot].reshape(2 * pair, cw)
+        to = lax.broadcasted_iota(jnp.int32, (pair, 2 * pair), 0)
+        of = lax.broadcasted_iota(jnp.int32, (pair, 2 * pair), 1)
+        mine = to + MOST * core + jnp.where(to >= MOST, MOST, 0)
+        pick = jnp.where(of == mine, 1.0, 0.0).astype(BF16)
+        keep(k, zz, jnp.dot(pick, both, preferred_element_type=F32))
 
     fsplit = 2
     fb = ff // fsplit
@@ -204,18 +303,74 @@
         act = gate / (1.0 + jnp.exp(-gate)) * up
         ht[pl.ds(pl.multiple_of(f0 * fb, 16), fb), pl.ds(pl.multiple_of(r0 * rb, 128), rb)] = act.astype(BF16)
 
-    def w_copy(other, slot):
-        return pltpu.make_async_remote_copy(
-            src_ref=w_all.at[:, slot], dst_ref=w_all.at[:, slot],
-            send_sem=ws.at[other], recv_sem=wr.at[slot],
+    def offset_peer(u, v):
+        return ((dp // side + u + side) % side) * side + (dp % side + v + side) % side
+
+    def w_copy(p, slot, half, u, v):
+        ref = w_all.at[p, slot]
+        if half is not None:
+            ref = w_all.at[p, slot, :, pl.ds(half * (width // 2), width // 2)]
+        return pltpu.make_async_remote_copy(
+            src_ref=ref, dst_ref=ref, send_sem=ws, recv_sem=wr.at[p, slot, half or 0],
+            device_id={"dp": offset_peer(u, v)}, device_id_type=MESH,
+        )
+
+    def w_hop(p, axis, slot, half, step):
+        along_x = (p == 0) == (axis == 0)
+        return w_copy(p, slot, half, step if along_x else 0, 0 if along_x else step)
+
+    def w_slot(p, u, v):
+        return offset_peer(u, v) if p == 0 else offset_peer(v, u)
+
+    def w_step(n):
+        for p in range(2):
+            if n == 0:
+                for axis in range(2):
+                    for step in (1, -1):
+                        w_hop(p, axis, dp, None, step).start()
+                continue
+            if n == 1:
+                for step in (1, -1):
+                    slot = w_slot(p, -step, 0)
+                    w_hop(p, 0, slot, None, step).wait_recv()
+                    w_hop(p, 0, slot, 0 if step == 1 else 1, step).start()
+                    for step2 in (1, -1):
+                        w_hop(p, 1, slot, None, step2).start()
+            if n == 2:
+                slot = w_slot(p, 2, 0)
+                for half in range(2):
+                    w_hop(p, 0, slot, half, 1).wait_recv()
+                for step2 in (1, -1):
+                    w_hop(p, 1, slot, None, step2).start()
+            for u in ((0,), (1, -1), (2,))[n - 1] if n < 4 else ():
+                for step in (1, -1):
+                    slot = w_slot(p, u, -step)
+                    w_hop(p, 1, slot, None, step).wait_recv()
+                    w_hop(p, 1, slot, 0 if step == 1 else 1, step).start()
+            if n == 4:
+                for u in (0, 1, -1, 2):
+                    for half in range(2):
+                        w_hop(p, 1, w_slot(p, u, 2), half, 1).wait_recv()
+
+    def w_sent():
+        ref = w_all.at[:, pl.ds(0, ndp - 1)]
+        pltpu.make_async_remote_copy(
+            src_ref=ref, dst_ref=ref, send_sem=ws, recv_sem=wr.at[0, 0, 0],
+            device_id={"dp": offset_peer(1, 0)}, device_id_type=MESH,
+        ).wait_send()
+
+    def r_copy(q, other):
+        return pltpu.make_async_remote_copy(
+            src_ref=ps.at[q, other], dst_ref=land.at[q, dp],
+            send_sem=ls_sem.at[q], recv_sem=lr_sem.at[q],
             device_id={"dp": other}, device_id_type=MESH,
         )
 
-    def r_copy(q, other, slot):
-        return pltpu.make_async_remote_copy(
-            src_ref=ps.at[q, other], dst_ref=land.at[q, slot],
-            send_sem=ls_sem.at[q, other], recv_sem=lr_sem.at[q, slot],
-            device_id={"dp": other}, device_id_type=MESH,
+    def r_all(q):
+        return pltpu.make_async_remote_copy(
+            src_ref=ps.at[q, pl.ds(0, ndp - 1)], dst_ref=land.at[q, pl.ds(0, ndp - 1)],
+            send_sem=ls_sem.at[q], recv_sem=lr_sem.at[q],
+            device_id={"dp": offset_peer(1, 0)}, device_id_type=MESH,
         )
 
     def partial(q):
@@ -227,96 +382,106 @@
             ps[q, f0 * per : (f0 + 1) * per] = part.astype(BF16).reshape(per, fd, cw)
         land[q, dp] = ps[q, dp]
 
-        @pl.loop(1, ndp)
-        def _(d):
-            r_copy(q, (dp + d) % ndp, dp).start()
-
-    x_done = max(OFFSETS) + hops
-
-    @pl.loop(0, 2 * hops + max(OFFSETS) + 1)
+        for u, v in PEER_ORDER:
+            r_copy(q, offset_peer(u, v)).start()
+
+    def lane(j, r, work):
+        period = hops + C_START[j]
+        h = r % period
+
+        @pl.when((r >= 0) & (r < 2 * period) & (h < hops))
+        def _():
+            work(j + NQ * (r // period), h)
+
+    def compute(j, r):
+        def work(k, h):
+            pairs(k, j % 2, h, functools.partial(select, k), functools.partial(select_packed, k))
+
+        lane(j, r, work)
+
+        @pl.when(r == 2 * hops + C_START[j] - 1)
+        def _():
+            partial(j)
+
+    @pl.loop(0, 2 * hops + max(C_START) + 1)
     def _(r):
         @pl.when(r < hops)
         def _():
             event(None, 0, r, lambda: None)
 
+        for direction in range(2):
+            for long in range(2):
+                h = nz // 2 - 3 + long
+
+                @pl.when(r == h)
+                def _():
+                    build_pack(direction, long, zslot(-h if direction == 0 else h))
+
         for j in range(NQ):
-            lr = r - OFFSETS[j]
-
-            @pl.when((lr >= 0) & (lr < 2 * hops))
+            lane(j, r, lambda k, h: event(k, j % 2, h, lambda: load(k, 0, j).wait()))
+            compute((j + 2) % NQ, r if j >= 2 else r - 1)
+            lane(j, r, lambda k, h: send_packed(k, j % 2, h))
+
+            if j == 1:
+                @pl.when(r < hops)
+                def _():
+                    pairs(None, 0, r, build, None)
+
+        for n in range(4):
+            @pl.when(r == n)
             def _():
-                second = lr // hops
-                k = j + NQ * second
-                event(k, j % 2, lr % hops, lambda: load(k, 0, j).wait())
-
-        @pl.when(r == 0)
-        def _():
-            w_load.wait()
-
-            @pl.loop(1, ndp)
-            def _(d):
-                w_copy((dp + d) % ndp, dp).start()
-
-        @pl.when(r == x_done + 1)
-        def _():
-            @pl.loop(1, ndp)
-            def _(d):
-                other = (dp + d) % ndp
-                w_copy(other, other).wait_recv()
-
-        @pl.when((r > x_done) & (r <= x_done + pieces))
-        def _():
-            hidden_piece(r - x_done - 1)
-
-        @pl.when((r >= 1) & (r <= hops))
-        def _():
-            pairs(None, 0, r - 1, build)
-
-        for j in range(NQ):
-            late = r - 1 - OFFSETS[j]
-
-            @pl.when((late >= 0) & (late < 2 * hops))
-            def _():
-                k = j + NQ * (late // hops)
-                pairs(k, j % 2, late % hops, functools.partial(select, k))
-
-            @pl.when(late == 2 * hops - 1)
-            def _():
-                partial(j)
+                if n == 0:
+                    w_load.wait()
+                w_step(n)
+
+        @pl.when(r == hops + 1)
+        def _():
+            w_step(4)
+
+        @pl.when((r > hops) & (r <= hops + pieces))
+        def _():
+            hidden_piece(r - hops - 1)
+
+    def ring_sent(k, parity):
+        for direction in range(2):
+            count = pl.ds(0, full_reach(k, parity, direction))
+            ref = g_all.at[count] if k is None else buf.at[k, count]
+            pltpu.make_async_remote_copy(
+                src_ref=ref, dst_ref=ref, send_sem=rs.at[sidx(k), direction],
+                recv_sem=rr.at[sidx(k), direction, 0],
+                device_id={"expert": partner}, device_id_type=MESH,
+            ).wait_send()
+        ref = g_all.at[pl.ds(0, nz)] if k is None else buf.at[k, pl.ds(0, nz - 4)]
+        pltpu.make_async_remote_copy(
+            src_ref=ref, dst_ref=ref, send_sem=psd.at[sidx(k)], recv_sem=pr.at[sidx(k), 0],
+            device_id={"expert": partner}, device_id_type=MESH,
+        ).wait_send()
+
+    def packed_sent(k, parity):
+        for direction in range(2):
+            packed_first(k, parity, direction).wait_send()
+            packed_second(k, parity, direction).wait_send()
+        ref = pin.at[k, 0, pl.ds(0, 2)]
+        pltpu.make_async_remote_copy(
+            src_ref=ref, dst_ref=ref, send_sem=pps.at[k], recv_sem=pr.at[k, 0],
+            device_id={"expert": partner}, device_id_type=MESH,
+        ).wait_send()
+
+    ring_sent(None, 0)
+    for k in range(items):
+        ring_sent(k, k % 2)
+        packed_sent(k, k % 2)
+    w_sent()
 
     for q in range(NQ):
-        @pl.loop(1, ndp)
-        def _(d):
-            other = (dp + d) % ndp
-            r_copy(q, other, other).wait_recv()
-
+        r_all(q).wait_recv()
         total = land[q, 0].astype(F32)
         for i in range(1, ndp):
             total = total + land[q, i].astype(F32)
         grad_ref[:, q * cw : (q + 1) * cw] = total
 
-    def drain(k, parity):
-        for direction in range(2):
-            @pl.loop(0, reach(parity, direction))
-            def _(h):
-                ring_copy(k, direction, me, h).wait_send()
-
-        @pl.loop(0, nz)
-        def _(zz):
-            partner_copy(k, me, zz).wait_send()
-
-    drain(None, 0)
-
-    @pl.loop(0, items // 2)
-    def _(half):
-        for parity in range(2):
-            drain(2 * half + parity, parity)
-
-    @pl.loop(1, ndp)
-    def _(d):
-        other = (dp + d) % ndp
-        w_copy(other, dp).wait_send()
-        for q in range(NQ):
-            r_copy(q, other, dp).wait_send()
+    for q in range(NQ):
+        r_all(q).wait_send()
 
 
 def grad_kernel(mesh, tokens, cotangent, routes_t, gates_t, weight):
@@ -347,15 +512,21 @@
             pltpu.VMEM((ndp * fd, nrows), BF16),
             pltpu.VMEM((NQ, ndp, fd, cw), BF16),
             pltpu.VMEM((NQ, ndp, fd, cw), BF16),
+            pltpu.VMEM((2, 2, 4 * MOST, toks), BF16),
+            pltpu.VMEM((items, 2, 2, 2 * MOST, cw), BF16),
+            pltpu.VMEM((items, 2, 3, 2, 2 * MOST, cw), BF16),
             dma((items + 1,)),
             dma((items + 1, 2, hops)),
-            dma((items + 1, 2, hops)),
+            dma((items + 1, 2)),
             dma((items + 1, nz)),
-            dma((items + 1, nz)),
-            dma((ndp,)),
-            dma((ndp,)),
-            dma((NQ, ndp)),
-            dma((NQ, ndp)),
+            dma((items + 1,)),
+            dma((2, ndp, 2)),
+            dma,
+            dma((NQ,)),
+            dma((NQ,)),
+            dma((items, 2)),
+            dma((items, 2)),
+            dma((items,)),
         ],
         compiler_params=pltpu.CompilerParams(
             collective_id=0, has_side_effects=True, vmem_limit_bytes=67043328

time: 263 us -> 203 us (0.77); the launches traced: 258 us -> 203 us
  Pallas kernels: 255 us -> 200 us
    pallas_call x1, Pallas kernels: 255 us -> 200 us  [grad_kernel(): pl.pallas_call(functools.partial(kernel, ndp, ne), out_shape=jax.ShapeDty...]
where the time goes in v2:
time: 203 us
  Pallas kernels  200 us (99%)
  other arithmetic  2.62 us (1%)
    pallas_call x1, Pallas kernels, grad_kernel(): pl.pallas_call(functools.partial(kernel, ndp, ne), out_shape=jax.ShapeDty...  200 us

profile of v2, /device:TPU:1, one launch (start us, length us, event | category | flops | bytes accessed | tf_op | source)
XLA Modules:
  0.0 203.3 jit_solution(1070372804443070325)
XLA Ops:
  0.6 200.0 %expert_grad.1 = f32[48,2048]{1,0:T(8,128)} custom-call(bf16[128,2048]{1,0:T(8,128)(2,1)} %x_ref.1, bf16[128,2048]{1,0:T(8,128)(2,1)} %c_ref.1, s32[8,128]{1,0:T(8,128)} %bitcast.35, f32[8,128]{1,0:T(8,128)} %bitcast.36, bf16[2,48,2048]{2,1,0:T(8,128)(2,1)} %bitcast.34), custom_call_target="tpu_custom_call" | custom-call | tf_op jit(solution)/shard_map/expert_grad/pallas_call | solution.py:500
  200.7 2.6 %fusion.5 = (f32[1,48,2048]{2,1,0:T(8,128)}, f32[1,48,2048]{2,1,0:T(8,128)}, f32[1,48,2048]{2,1,0:T(8,128)}) fusion(f32[48,2048]{1,0:T(8,128)} %expert_grad.1, f32[1,48,2048]{2,1,0:T(8,128)} %param.15, f32[1,48,2048]{2,1,0:T(8,128)} %param.14, f32[1,48,2048]{2,1,0:T(8,128)} %param.13), kind=kLoop, calls=%fused_computation.9 | loop fusion | flops 1277952 | bytes 2752512 | tf_op jit(solution)/shard_map/broadcast_in_dim | solution.py:551

commit v3 on v2

--- a/solution.py
+++ b/solution.py
@@ -9,7 +9,7 @@
 
 MOST = 24
 NQ = 4
-C_START = (0, 1, 3, 5)
+LAG = 1
 SIDE = 4
 PEER_ORDER = (
     (0, 1), (1, 0), (0, -1), (-1, 0), (1, 1), (-1, -1), (1, -1), (-1, 1),
@@ -61,10 +61,9 @@
             src.at[:, pl.ds(q * cw, cw)], buf.at[k, me], loc_sem.at[k]
         )
 
-    for q in range(NQ):
-        load(q, 0, q).start()
-    for q in range(NQ):
-        load(NQ + q, 1, q).start()
+    for t in range(2):
+        for q in range(NQ):
+            load(t * NQ + q, t, q).start()
     w_load = pltpu.make_async_copy(w_ref, w_all.at[:, dp], loc_sem.at[items])
     w_load.start()
 
@@ -385,27 +384,36 @@
         for u, v in PEER_ORDER:
             r_copy(q, offset_peer(u, v)).start()
 
-    def lane(j, r, work):
-        period = hops + C_START[j]
-        h = r % period
-
-        @pl.when((r >= 0) & (r < 2 * period) & (h < hops))
-        def _():
-            work(j + NQ * (r // period), h)
-
-    def compute(j, r):
-        def work(k, h):
-            pairs(k, j % 2, h, functools.partial(select, k), functools.partial(select_packed, k))
-
-        lane(j, r, work)
-
-        @pl.when(r == 2 * hops + C_START[j] - 1)
-        def _():
-            partial(j)
-
-    @pl.loop(0, 2 * hops + max(C_START) + 1)
-    def _(r):
-        @pl.when(r < hops)
+    lanes = items // 2
+    c_start = max(hops - 4, 4)
+
+    def begin(k):
+        return (k // NQ) * (c_start + ((k - NQ) * 2))
+
+    last_round = c_start + ((NQ - 1) * 2) + hops
+
+    def each(g, work):
+        for parity in range(2):
+            k = 2 * (g % lanes) + parity
+            h = g // lanes - begin(k)
+
+            @pl.when((g >= 0) & (h >= 0) & (h < hops))
+            def _():
+                work(k, parity, h)
+
+    def compute(k, parity, h):
+        pairs(k, parity, h, functools.partial(select, k), functools.partial(select_packed, k))
+
+        @pl.when((h == hops - 1) & (k >= NQ))
+        def _():
+            partial(k - NQ)
+
+    @pl.loop(0, last_round * lanes + LAG)
+    def _(g):
+        r = g // lanes
+        m = g % lanes
+
+        @pl.when((m == 0) & (r < hops))
         def _():
             event(None, 0, r, lambda: None)
 
@@ -413,34 +421,35 @@
             for long in range(2):
                 h = nz // 2 - 3 + long
 
-                @pl.when(r == h)
+                @pl.when((m == 0) & (r == h))
                 def _():
                     build_pack(direction, long, zslot(-h if direction == 0 else h))
 
-        for j in range(NQ):
-            lane(j, r, lambda k, h: event(k, j % 2, h, lambda: load(k, 0, j).wait()))
-            compute((j + 2) % NQ, r if j >= 2 else r - 1)
-            lane(j, r, lambda k, h: send_packed(k, j % 2, h))
-
-            if j == 1:
-                @pl.when(r < hops)
-                def _():
-                    pairs(None, 0, r, build, None)
+        each(g, lambda k, parity, h: event(k, parity, h, lambda: load(k, 0, 0).wait()))
+
+        @pl.when((m == LAG) & (r < hops))
+        def _():
+            pairs(None, 0, r, build, None)
+
+        each(g - LAG, compute)
+        each(g, send_packed)
 
         for n in range(4):
-            @pl.when(r == n)
+            @pl.when((m == lanes - 1) & (r == n))
             def _():
                 if n == 0:
                     w_load.wait()
                 w_step(n)
 
-        @pl.when(r == hops + 1)
+        @pl.when((m == lanes // 2 - 1) & (r == hops + 1))
         def _():
             w_step(4)
 
-        @pl.when((r > hops) & (r <= hops + pieces))
-        def _():
-            hidden_piece(r - hops - 1)
+        piece = 2 * (r - hops - 1) + m // (lanes // 2)
+
+        @pl.when((m % (lanes // 2) == lanes // 2 - 1) & (r > hops) & (piece < pieces))
+        def _():
+            hidden_piece(piece)
 
     def ring_sent(k, parity):
         for direction in range(2):
@@ -468,19 +477,25 @@
         ).wait_send()
 
     ring_sent(None, 0)
-    for k in range(items):
-        ring_sent(k, k % 2)
-        packed_sent(k, k % 2)
+
+    @pl.loop(0, lanes)
+    def _(m):
+        for parity in range(2):
+            ring_sent(2 * m + parity, parity)
+            packed_sent(2 * m + parity, parity)
+
     w_sent()
 
-    for q in range(NQ):
+    @pl.loop(0, NQ)
+    def _(q):
         r_all(q).wait_recv()
         total = land[q, 0].astype(F32)
         for i in range(1, ndp):
             total = total + land[q, i].astype(F32)
-        grad_ref[:, q * cw : (q + 1) * cw] = total
-
-    for q in range(NQ):
+        grad_ref[:, pl.ds(pl.multiple_of(q * cw, 128), cw)] = total
+
+    @pl.loop(0, NQ)
+    def _(q):
         r_all(q).wait_send()
 
 

time: 203 us -> 200 us (0.985)
  Pallas kernels: 200 us -> 197 us
    pallas_call x1, Pallas kernels: 200 us -> 197 us  [grad_kernel(): pl.pallas_call(functools.partial(kernel, ndp, ne), out_shape=jax.ShapeDty...]
where the time goes in v3:
time: 200 us
  Pallas kernels  197 us (98%)
  other arithmetic  2.62 us (1%)
    pallas_call x1, Pallas kernels, grad_kernel(): pl.pallas_call(functools.partial(kernel, ndp, ne), out_shape=jax.ShapeDty...  197 us

profile of v3, /device:TPU:1, one launch (start us, length us, event | category | flops | bytes accessed | tf_op | source)
XLA Modules:
  0.0 199.8 jit_solution(6685078755102978473)
XLA Ops:
  0.6 196.6 %expert_grad.1 = f32[48,2048]{1,0:T(8,128)} custom-call(bf16[128,2048]{1,0:T(8,128)(2,1)} %x_ref.1, bf16[128,2048]{1,0:T(8,128)(2,1)} %c_ref.1, s32[8,128]{1,0:T(8,128)} %bitcast.35, f32[8,128]{1,0:T(8,128)} %bitcast.36, bf16[2,48,2048]{2,1,0:T(8,128)(2,1)} %bitcast.34), custom_call_target="tpu_custom_call" | custom-call | tf_op jit(solution)/shard_map/expert_grad/pallas_call | solution.py:515
  197.2 2.6 %fusion.5 = (f32[1,48,2048]{2,1,0:T(8,128)}, f32[1,48,2048]{2,1,0:T(8,128)}, f32[1,48,2048]{2,1,0:T(8,128)}) fusion(f32[48,2048]{1,0:T(8,128)} %expert_grad.1, f32[1,48,2048]{2,1,0:T(8,128)} %param.15, f32[1,48,2048]{2,1,0:T(8,128)} %param.14, f32[1,48,2048]{2,1,0:T(8,128)} %param.13), kind=kLoop, calls=%fused_computation.9 | loop fusion | flops 1277952 | bytes 2752512 | tf_op jit(solution)/shard_map/broadcast_in_dim | solution.py:566

commit v4 on v3

--- a/solution.py
+++ b/solution.py
@@ -11,10 +11,6 @@
 NQ = 4
 LAG = 1
 SIDE = 4
-PEER_ORDER = (
-    (0, 1), (1, 0), (0, -1), (-1, 0), (1, 1), (-1, -1), (1, -1), (-1, 1),
-    (0, 2), (2, 0), (1, 2), (2, 1), (-1, 2), (2, -1), (2, 2),
-)
 
 BETA_ONE = 0.9
 BETA_TWO = 0.95
@@ -373,16 +369,20 @@
         )
 
     def partial(q):
-        for f0 in range(fsplit):
-            part = jnp.dot(
-                ht[f0 * fb : (f0 + 1) * fb, :], rows[NQ + q], preferred_element_type=F32
-            )
-            per = ndp // fsplit
-            ps[q, f0 * per : (f0 + 1) * per] = part.astype(BF16).reshape(per, fd, cw)
+        bl = side * fd
+        for f in range(1, side + 2):
+            if f <= side:
+                row = (dp // side + f) % side
+                part = jnp.dot(
+                    ht[pl.ds(pl.multiple_of(row * bl, 16), bl), :], rows[NQ + q],
+                    preferred_element_type=F32,
+                )
+                ps[q, pl.ds(row * side, side)] = part.astype(BF16).reshape(side, fd, cw)
+            if f > 1:
+                for v in (1, 2, 3, 0):
+                    if f <= side or v:
+                        r_copy(q, offset_peer((f - 1) % side, v)).start()
         land[q, dp] = ps[q, dp]
-
-        for u, v in PEER_ORDER:
-            r_copy(q, offset_peer(u, v)).start()
 
     lanes = items // 2
     c_start = max(hops - 4, 4)

time: 200 us -> 200 us (level)
  no operation moved by 1% of the time
where the time goes in v4:
time: 200 us
  Pallas kernels  197 us (98%)
  other arithmetic  2.62 us (1%)
    pallas_call x1, Pallas kernels, grad_kernel(): pl.pallas_call(functools.partial(kernel, ndp, ne), out_shape=jax.ShapeDty...  197 us

profile of v4, /device:TPU:1, one launch (start us, length us, event | category | flops | bytes accessed | tf_op | source)
XLA Modules:
  0.0 200.2 jit_solution(11518792387940153508)
XLA Ops:
  0.6 196.9 %expert_grad.1 = f32[48,2048]{1,0:T(8,128)} custom-call(bf16[128,2048]{1,0:T(8,128)(2,1)} %x_ref.1, bf16[128,2048]{1,0:T(8,128)(2,1)} %c_ref.1, s32[8,128]{1,0:T(8,128)} %bitcast.35, f32[8,128]{1,0:T(8,128)} %bitcast.36, bf16[2,48,2048]{2,1,0:T(8,128)(2,1)} %bitcast.34), custom_call_target="tpu_custom_call" | custom-call | tf_op jit(solution)/shard_map/expert_grad/pallas_call | solution.py:515
  197.5 2.6 %fusion.5 = (f32[1,48,2048]{2,1,0:T(8,128)}, f32[1,48,2048]{2,1,0:T(8,128)}, f32[1,48,2048]{2,1,0:T(8,128)}) fusion(f32[48,2048]{1,0:T(8,128)} %expert_grad.1, f32[1,48,2048]{2,1,0:T(8,128)} %param.15, f32[1,48,2048]{2,1,0:T(8,128)} %param.14, f32[1,48,2048]{2,1,0:T(8,128)} %param.13), kind=kLoop, calls=%fused_computation.9 | loop fusion | flops 1277952 | bytes 2752512 | tf_op jit(solution)/shard_map/broadcast_in_dim | solution.py:566
